TPU v7x, 32 devices: a whole 2x2x4 slice. The times are simulated.
32 devices in a mesh: ctx: 4 (over z), exp: 4 (over y, x), head: 2 (over core).
Axes of the slice: x: 2, y: 2, z: 4, core: 2. Of those that a mesh axis runs over, the one named last changes fastest.
Arguments:
- queries: bfloat16 [2048, 2048], P(('ctx', 'exp'), 'head'), may hold values from -6 to 6
- keys: bfloat16 [2048, 256], P(('ctx', 'exp'), 'head'), may hold values from -6 to 6
- values: bfloat16 [2048, 256], P(('ctx', 'exp'), 'head'), may hold values from -12 to 12
- residual: bfloat16 [2048, 2880], P(('ctx', 'exp', 'head')), may hold values from -48 to 48
- out_projection: bfloat16 [2048, 2880], P('head', 'exp'), may hold values from -0.125 to 0.125
- norm_gain: float32 [2880], replicated, may hold values from 0.25 to 1.75
- route_ids: int32 [2048, 4], P(('ctx', 'exp', 'head')), may hold values from 0 to 7, all different within a row; in each aligned block of 64 rows (0 to 63, 64 to 127, ...) at most 64 rows name the same one
- route_weights: float32 [2048, 4], P(('ctx', 'exp', 'head')), may hold values from 0.05 to 1
- w_gate: bfloat16 [8, 2880, 1536], P(('ctx', 'head'), None, 'exp'), may hold values from -0.109375 to 0.109375
- w_up: bfloat16 [8, 2880, 1536], P(('ctx', 'head'), None, 'exp'), may hold values from -0.109375 to 0.109375
- w_down: bfloat16 [8, 1536, 2880], P(('ctx', 'head'), 'exp'), may hold values from -0.15625 to 0.15625
Outputs:
- mixed: bfloat16 [2048, 2880], P(('ctx', 'exp', 'head'))
Inputs may be any that keep to these rules, and one draw needn't show every extreme that they name: `route_ids`: each row names 4 different experts. In the rows of one device (aligned blocks of 64 rows) no expert is named by more than 64 rows, a bound that some block reaches.
All inputs are finite; a program needn't handle non-finite values.
Results may differ from a plain program's by a relative error of at most 0.0037.
Values may be sent and summed in bfloat16 or wider, within the bound.
No kernel may reach another device: no remote copies, remote signals or barrier semaphores. Data moves between devices by JAX's collectives and lax.ppermute only.
A program may use at most 128 MiB of HBM per device.

v0:
```python
import jax
import jax.numpy as jnp
from jax import lax
from jax.sharding import PartitionSpec as P

D = 2880
QUERY_HEADS = 32
KEY_VALUE_HEADS = 4
HEAD_DIMENSION = 64
BAND_WIDTH_KEYS = 128
TOP = 4
EPSILON = 1e-05
SLOPE = 1.702


def from_behind(x, axis, by):
    devices = lax.axis_size(axis)
    pairs = [(i, i + by) for i in range(devices) if 0 <= i + by < devices]
    return lax.ppermute(x, axis, pairs)


def attend_band(
    queries, concatenated_keys, concatenated_values, window, head_size, group, anchor_position
):
    tokens = queries.shape[0]
    block = min(tokens, 512)
    count = tokens // block
    heads = queries.shape[1] // head_size
    kv_heads = heads // group
    scale = head_size ** (-0.5)

    def one_block(index):
        begin = index * block
        query_part = queries.reshape(block, kv_heads, group, head_size)
        key_part = concatenated_keys.reshape(block + window, kv_heads, head_size)
        value_part = concatenated_values.reshape(block + window, kv_heads, head_size)
        scores = (
            jnp.einsum("qgjd,kgd->gjqk", query_part, key_part, preferred_element_type=jnp.float32)
            * scale
        )
        query_pos = anchor_position + begin + jnp.arange(block, dtype=jnp.int32)
        key_pos = anchor_position - window + begin + jnp.arange(block + window, dtype=jnp.int32)
        distance = query_pos[:, None] - key_pos[None, :]
        allowed = (distance >= 0) & (distance < window) & (key_pos[None, :] >= 0)
        scores = jnp.where(allowed, scores, -jnp.inf)
        highest = jnp.max(scores, axis=-1, keepdims=True)
        weights = jnp.exp(scores - highest)
        weights = (weights / jnp.sum(weights, axis=-1, keepdims=True)).astype(jnp.bfloat16)
        result = jnp.einsum(
            "gjqk,kgd->qgjd", weights, value_part, preferred_element_type=jnp.float32
        )
        return result.astype(jnp.bfloat16).reshape(block, heads * head_size)

    outputs = lax.map(one_block, jnp.arange(count, dtype=jnp.int32))
    return outputs.reshape(tokens, heads * head_size)


def expert_rows(inputs, gate_slice, up_slice, down_slice):
    gate = jnp.dot(inputs, gate_slice, preferred_element_type=jnp.float32)
    upward = jnp.dot(inputs, up_slice, preferred_element_type=jnp.float32)
    active = ((upward + 1.0) * gate * jax.nn.sigmoid(SLOPE * gate)).astype(jnp.bfloat16)
    return jnp.dot(active, down_slice, preferred_element_type=jnp.float32)


def local(
    queries,
    keys,
    values,
    residual,
    out_projection,
    norm_gain,
    route_ids,
    route_weights,
    w_gate,
    w_up,
    w_down,
):
    tokens = queries.shape[0]
    key_band_extent = keys.shape[1]
    stacked = jnp.concatenate([keys, values], axis=1)
    prior = from_behind(stacked, ("ctx", "exp"), 1)
    joined_heads = jnp.concatenate([prior, stacked], axis=0)
    anchor_position = lax.axis_index(("ctx", "exp")) * tokens
    attended_rows = attend_band(
        queries,
        joined_heads[:, :key_band_extent],
        joined_heads[:, key_band_extent:],
        BAND_WIDTH_KEYS,
        HEAD_DIMENSION,
        QUERY_HEADS // KEY_VALUE_HEADS,
        anchor_position,
    )
    partial_sum = jnp.dot(
        attended_rows,
        lax.all_gather(out_projection, "exp", axis=1, tiled=True),
        preferred_element_type=jnp.float32,
    )
    attn_out = lax.psum_scatter(partial_sum, "head", scatter_dimension=0, tiled=True)
    hidden_state = residual.astype(jnp.float32) + attn_out
    mean_square = jnp.mean(hidden_state * hidden_state, axis=1, keepdims=True)
    normed = (hidden_state * lax.rsqrt(mean_square + EPSILON) * norm_gain[None, :]).astype(
        jnp.bfloat16
    )
    local_rows = normed.shape[0]
    experts = lax.axis_size("ctx") * lax.axis_size("head")
    capacity = max(2, TOP * tokens // experts)
    flat_ids = route_ids.reshape(-1)
    one_hot = (flat_ids[:, None] == jnp.arange(experts, dtype=jnp.int32)[None, :]).astype(jnp.int32)
    earlier = jnp.cumsum(one_hot, axis=0) - one_hot
    rank = jnp.sum(earlier * one_hot, axis=1)
    slot = flat_ids * capacity + rank
    outgoing = (
        jnp.zeros((experts * capacity, D), jnp.bfloat16)
        .at[slot]
        .set(jnp.repeat(normed, TOP, axis=0))
    )
    outgoing = outgoing.reshape(experts, capacity, D)
    arrived = lax.all_to_all(outgoing, ("ctx", "head"), split_axis=0, concat_axis=0, tiled=True)
    pooled = lax.all_gather(arrived, "exp", axis=0, tiled=True)
    partial_rows = expert_rows(
        pooled.reshape(experts * lax.axis_size("exp") * capacity, D), w_gate[0], w_up[0], w_down[0]
    )
    summed = lax.psum_scatter(
        partial_rows.reshape(experts * lax.axis_size("exp"), capacity, D),
        "exp",
        scatter_dimension=0,
        tiled=True,
    ).astype(jnp.bfloat16)
    returned = lax.all_to_all(summed, ("ctx", "head"), split_axis=0, concat_axis=0, tiled=True)
    flat_back = returned.reshape(experts * capacity, D)
    picked = flat_back[slot].astype(jnp.float32).reshape(local_rows, TOP, D)
    moe = jnp.sum(picked * route_weights[:, :, None], axis=1)
    return (hidden_state + moe).astype(jnp.bfloat16)


def solution(mesh):
    return jax.shard_map(
        local,
        mesh=mesh,
        in_specs=(
            P(("ctx", "exp"), "head"),
            P(("ctx", "exp"), "head"),
            P(("ctx", "exp"), "head"),
            P(("ctx", "exp", "head"), None),
            P("head", "exp"),
            P(),
            P(("ctx", "exp", "head"), None),
            P(("ctx", "exp", "head"), None),
            P(("ctx", "head"), None, "exp"),
            P(("ctx", "head"), None, "exp"),
            P(("ctx", "head"), "exp", None),
        ),
        out_specs=P(("ctx", "exp", "head"), None),
        check_vma=False,
    )
```

profile of v0, /device:TPU:0, one launch (start us, length us, event | category | flops | bytes accessed | tf_op | source)
XLA Modules:
  0.0 637.0 jit_solution(17359367700430694004)
XLA Ops:
  8.8 4.9 collective-permute-start
  13.9 1.1 copy.27
  16.6 1.1 convolution_convert_fusion
  17.7 61.0 %all-gather.3.cloned.1.call-done = bf16[1024,2880]{0,1:T(8,128)(2,1)} async-done(((bf16[1024,720]{0,1:T(8,128)(2,1)}), bf16[1024,2880]{0,1:T(8,128)(2,1)}) %all-gather.3.cloned.1.call-update) | async-done | bytes 5898256 | tf_op jit(solution)/shard_map/all_gather | solution.py:95
  78.7 6.0 fusion.27
  86.2 7.6 %reduce-scatter.3.cloned.1.call-done = f32[64,2880]{1,0:T(8,128)} async-done(((f32[128,2880]{1,0:T(8,128)}), f32[64,2880]{1,0:T(8,128)}) %reduce-scatter.3.cloned.1.call-update) | async-done | bytes 737296 | tf_op jit(solution)/shard_map/reduce_scatter | solution.py:98
  93.8 1.3 multiply_reduce_fusion.1
  95.2 1.3 multiply_convert_fusion.1
  96.4 1.5 broadcast_in_dim.38
  98.0 3.6 reshape.129
  101.5 5.6 scatter_custom_fusion
  107.1 73.8 %all_to_all.10 = bf16[8,64,2880]{2,1,0:T(8,128)(2,1)} all-to-all(bf16[8,64,2880]{2,1,0:T(8,128)(2,1)} %bitcast.60), channel_id=1, replica_groups=mesh['ctx'=4,'exp'=4,'head'=2] {'ctx','head'}, dimensions={0} | all-to-all | bytes 5898240 | tf_op jit(solution)/shard_map/all_to_all | solution.py:118
  181.1 116.8 %all-gather.5.cloned.1.call-done = bf16[32,64,2880]{2,1,0:T(8,128)(2,1)} async-done(((bf16[8,64,2880]{2,1,0:T(8,128)(2,1)}), bf16[32,64,2880]{2,1,0:T(8,128)(2,1)}) %all-gather.5.cloned.1.call-update) | async-done | bytes 11796496 | tf_op jit(solution)/shard_map/all_gather | solution.py:119
  298.0 10.6 %fusion.3 = f32[2048,384]{1,0:T(8,128)S(1)} fusion(bf16[2048,2880]{1,0:T(8,128)(2,1)} %bitcast.71, bf16[1,2880,384]{2,1,0:T(8,128)(2,1)} %param.19), kind=kOutput, calls=%fused_computation.7 | convolution fusion | flops 4529848320 | bytes 17154048 | tf_op jit(solution)/shard_map/dot_general | solution.py:59
  308.6 7.3 %multiply_convert_fusion = bf16[2048,384]{1,0:T(8,128)(2,1)S(1)} fusion(f32[2048,384]{1,0:T(8,128)S(1)} %fusion.3, bf16[2048,2880]{1,0:T(8,128)(2,1)S(1)} %bitcast.72, bf16[1,2880,384]{2,1,0:T(8,128)(2,1)S(1)} %copy-done.8), kind=kOutput, calls=%fused_computation.3 | convolution fusion | flops 4536139776 | bytes 18726912 | tf_op jit(solution)/shard_map/dot_general | solution.py:60
  315.9 11.4 %fusion.1 = f32[32,64,2880]{2,1,0:T(8,128)} fusion(bf16[32,64,384]{2,1,0:T(8,128)(2,1)S(1)} %bitcast.61, bf16[1,384,2880]{1,2,0:T(8,128)(2,1)S(1)} %copy-done), kind=kOutput, calls=%fused_computation.5 | convolution fusion | flops 4529848320 | bytes 27377664 | tf_op jit(solution)/shard_map/dot_general | solution.py:62
  327.3 213.4 %reduce-scatter.5.cloned.1.call-done = f32[8,64,2880]{2,1,0:T(8,128)} async-done(((f32[32,64,2880]{2,1,0:T(8,128)}), f32[8,64,2880]{2,1,0:T(8,128)}) %reduce-scatter.5.cloned.1.call-update) | async-done | bytes 5898256 | tf_op jit(solution)/shard_map/reduce_scatter | solution.py:123
  540.7 4.8 convert_element_type.48
  545.4 4.7 all-to-all-start.1
  550.3 68.6 %all-to-all-done.1 = bf16[8,64,2880]{2,1,0:T(8,128)(2,1)S(1)} async-done(((bf16[8,64,2880]{2,1,0:T(8,128)(2,1)}), bf16[8,64,2880]{2,1,0:T(8,128)(2,1)S(1)}, u32[]{:S(2)}, u32[]{:S(2)}) %all-to-all-start.1) | async-done | bytes 2949152 | tf_op jit(solution)/shard_map/all_to_all | solution.py:129
  618.9 2.7 gather_fusion
  621.5 4.1 reshape.116
  625.6 4.0 multiply_reduce_fusion
  629.6 0.9 add_convert_fusion
  (53 shorter events, 5.9 us)
Async XLA Ops:
  6.5 309.3 %copy-start = (bf16[1,384,2880]{1,2,0:T(8,128)(2,1)S(1)}, bf16[1,384,2880]{1,2,0:T(8,128)(2,1)}, u32[]{:S(2)}) copy-start(bf16[1,384,2880]{1,2,0:T(8,128)(2,1)} %param.21) | copy-start | bytes 6635524
  6.5 72.2 %all-gather.3.cloned.1.call-start = ((), (), s32[]{:S(2)}) async-start(), calls=%async_computation.4 | async-start | bytes 7372800 | tf_op jit(solution)/shard_map/all_gather | solution.py:95
  7.3 86.6 %reduce-scatter.3.cloned.1.call-start = ((), (), s32[]{:S(2)}) async-start(), calls=%async_computation.5 | async-start | bytes 2260992 | tf_op jit(solution)/shard_map/reduce_scatter | solution.py:98
  8.8 6.8 %collective-permute-start = (bf16[128,256]{1,0:T(8,128)(2,1)S(1)}, bf16[128,256]{1,0:T(8,128)(2,1)S(1)}, u32[]{:S(2)}, u32[]{:S(2)}) collective-permute-start(bf16[128,256]{1,0:T(8,128)(2,1)S(1)} %constant_dynamic-update-slice_fusion), channel_id=1, source_target_pairs={{0,2},{2,4},{4,6},{6,8},{8,10},{10,12},{12,14},{14,16},{16,18},{18... | collective-permute-start | bytes 196616 | tf_op jit(solution)/shard_map/ppermute | solution.py:19
  78.7 6.1 copy-start.5
  78.7 15.1 %copy-start.3 = (bf16[64,2880]{1,0:T(8,128)(2,1)S(1)}, bf16[64,2880]{1,0:T(8,128)(2,1)}, u32[]{:S(2)}) copy-start(bf16[64,2880]{1,0:T(8,128)(2,1)} %param.14) | copy-start | bytes 1105924
  84.7 10.5 %copy-start.4 = (f32[2880]{0:T(1024)S(1)}, f32[2880]{0:T(1024)}, u32[]{:S(2)}) copy-start(f32[2880]{0:T(1024)} %param.16) | copy-start | bytes 34564
  84.7 213.3 %all-gather.5.cloned.1.call-start = ((), (), s32[]{:S(2)}) async-start(), calls=%async_computation.6 | async-start | bytes 15073280 | tf_op jit(solution)/shard_map/all_gather | solution.py:119
  180.9 359.7 %reduce-scatter.5.cloned.1.call-start = ((), (), s32[]{:S(2)}) async-start(), calls=%async_computation.7 | async-start | bytes 30146560 | tf_op jit(solution)/shard_map/reduce_scatter | solution.py:123
  298.0 10.6 %copy-start.7 = (bf16[32,64,2880]{2,1,0:T(8,128)(2,1)S(1)}, bf16[32,64,2880]{2,1,0:T(8,128)(2,1)}, u32[]{:S(2)}) copy-start(bf16[32,64,2880]{2,1,0:T(8,128)(2,1)} %all-gather.5.cloned.1.call-done) | copy-start | bytes 35389444
  298.0 10.6 %copy-start.8 = (bf16[1,2880,384]{2,1,0:T(8,128)(2,1)S(1)}, bf16[1,2880,384]{2,1,0:T(8,128)(2,1)}, u32[]{:S(2)}) copy-start(bf16[1,2880,384]{2,1,0:T(8,128)(2,1)} %param.20) | copy-start | bytes 6635524
  545.4 4.7 copy-start.6
  545.4 73.4 %all-to-all-start.1 = ((bf16[8,64,2880]{2,1,0:T(8,128)(2,1)}), bf16[8,64,2880]{2,1,0:T(8,128)(2,1)S(1)}, u32[]{:S(2)}, u32[]{:S(2)}) async-start(bf16[8,64,2880]{2,1,0:T(8,128)(2,1)} %convert_element_type.48), calls=%async_computation.3 | async-start | bytes 6029312 | tf_op jit(solution)/shard_map/all_to_all | solution.py:129
  621.5 8.9 %copy-start.1 = (bf16[1,384,2880]{1,2,0:T(8,128)(2,1)S(1)}, bf16[1,384,2880]{1,2,0:T(8,128)(2,1)}, u32[]{:S(2)}) copy-start(bf16[1,384,2880]{1,2,0:T(8,128)(2,1)} %param.21) | copy-start | bytes 6635524
  625.6 4.0 copy-start.2
Sparse Core Ops, SparseCore 0:
  9.2 69.4 all-gather.2
  84.8 8.9 reduce-scatter.2
  181.0 116.8 all-gather.4
  327.4 213.2 reduce-scatter.4
where the time goes:
time: 638 us; the launch traced here: 637 us
  waiting for transfers between devices  469 us (74%)
  blocking collectives  73.8 us (12%)
  matrix products  37.1 us (6%)
  local copies, waits for them, and re-layouts  21.2 us (3%)
  between operations  13.3 us (2%)
  other arithmetic  13.1 us (2%)
  starting transfers between devices  9.91 us (2%)
    reduce_scatter x1, waiting for transfers between devices, local(): lax.psum_scatter(partial_rows.reshape(experts * lax.axis_size('exp'), cap...  213 us
    all_gather x1, waiting for transfers between devices, local(): pooled = lax.all_gather(arrived, 'exp', axis=0, tiled=True)  117 us
    all_to_all x1, blocking collectives, local(): lax.all_to_all(outgoing, ('ctx', 'head'), split_axis=0, concat_axis=0, ti...  73.8 us
    all_to_all x1, waiting for transfers between devices, local(): lax.all_to_all(summed, ('ctx', 'head'), split_axis=0, concat_axis=0, tile...  68.6 us
    all_gather x1, waiting for transfers between devices, local(): lax.all_gather(out_projection, 'exp', axis=1, tiled=True)  61 us
  transfers between devices with their start and end apart: 6, of which 6 were waited for; matrix products, arithmetic and copies ran while one was open for 1% of the time, Pallas kernels for 0%

commit v1 on v0

--- a/solution.py
+++ b/solution.py
@@ -2,6 +2,7 @@
 import jax.numpy as jnp
 from jax import lax
 from jax.sharding import PartitionSpec as P
+from jax.lax import axis_index, ppermute, psum
 
 D = 2880
 QUERY_HEADS = 32
@@ -116,7 +117,18 @@
     )
     outgoing = outgoing.reshape(experts, capacity, D)
     arrived = lax.all_to_all(outgoing, ("ctx", "head"), split_axis=0, concat_axis=0, tiled=True)
-    pooled = lax.all_gather(arrived, "exp", axis=0, tiled=True)
+    all_values = psum(1, "exp")
+    p_next, y, piece_now = (all_values, axis_index("exp"), arrived.shape[0])
+    pooled = jnp.zeros(
+        (*arrived.shape[:0], p_next * piece_now, *arrived.shape[0 + 1 :]), arrived.dtype
+    )
+    item_now = arrived
+    table = [(j, (j + 1) % p_next) for j in range(p_next)]
+    for tick in [*range(p_next)]:
+        tile_out = (y - tick) % p_next
+        pooled = lax.dynamic_update_slice_in_dim(pooled, item_now, tile_out * piece_now, axis=0)
+        if tick < p_next - 1:
+            item_now = ppermute(item_now, "exp", table)
     partial_rows = expert_rows(
         pooled.reshape(experts * lax.axis_size("exp") * capacity, D), w_gate[0], w_up[0], w_down[0]
     )

time: 638 us -> 732 us (1.15)
  waiting for transfers between devices: 469 us -> 536 us
  local copies, waits for them, and re-layouts: 21.2 us -> 46.3 us
    ppermute x0 -> x3, waiting for transfers between devices: none -> 184 us  [local(): item_now = ppermute(item_now, 'exp', table)]
    all_gather x1 -> x0, waiting for transfers between devices: 117 us -> none  [local(): pooled = lax.all_gather(arrived, 'exp', axis=0, tiled=True)]
    dynamic_update_slice x0 -> x4, local copies, waits for them, and re-layouts: none -> 11.1 us  [local(): lax.dynamic_update_slice_in_dim(pooled, item_now, tile_out * piece_now, a...]
  transfers between devices with their start and end apart: 6 -> 8, of which waited for: 6 -> 8; matrix products, arithmetic and copies ran while one was open for 1% -> 3% of each run, Pallas kernels for 0% -> 0%
where the time goes in v1:
time: 732 us; the launch traced here: 731 us
  waiting for transfers between devices  536 us (73%)
  blocking collectives  73.7 us (10%)
  local copies, waits for them, and re-layouts  46.3 us (6%)
  matrix products  37.4 us (5%)
  between operations  13.3 us (2%)
  other arithmetic  13.2 us (2%)
  starting transfers between devices  11.8 us (2%)
    reduce_scatter x1, waiting for transfers between devices, local(): lax.psum_scatter(partial_rows.reshape(experts * lax.axis_size('exp'), cap...  213 us
    ppermute x3, waiting for transfers between devices, local(): item_now = ppermute(item_now, 'exp', table)  184 us
    all_to_all x1, blocking collectives, local(): lax.all_to_all(outgoing, ('ctx', 'head'), split_axis=0, concat_axis=0, ti...  73.7 us
    all_to_all x1, waiting for transfers between devices, local(): lax.all_to_all(summed, ('ctx', 'head'), split_axis=0, concat_axis=0, tile...  68.6 us
    all_gather x1, waiting for transfers between devices, local(): lax.all_gather(out_projection, 'exp', axis=1, tiled=True)  61 us
  transfers between devices with their start and end apart: 8, of which 8 were waited for; matrix products, arithmetic and copies ran while one was open for 3% of the time, Pallas kernels for 0%

profile of v1, /device:TPU:0, one launch (start us, length us, event | category | flops | bytes accessed | tf_op | source)
XLA Modules:
  0.0 731.1 jit_solution(11445882959898797913)
XLA Ops:
  8.8 4.9 collective-permute-start
  17.7 61.0 %all-gather.2.cloned.1.call-done = bf16[1024,2880]{0,1:T(8,128)(2,1)} async-done(((bf16[1024,720]{0,1:T(8,128)(2,1)}), bf16[1024,2880]{0,1:T(8,128)(2,1)}) %all-gather.2.cloned.1.call-update) | async-done | bytes 5898256 | tf_op jit(solution)/shard_map/all_gather | solution.py:96
  78.7 6.0 fusion.30
  86.2 7.6 %reduce-scatter.3.cloned.1.call-done = f32[64,2880]{1,0:T(8,128)} async-done(((f32[128,2880]{1,0:T(8,128)}), f32[64,2880]{1,0:T(8,128)}) %reduce-scatter.3.cloned.1.call-update) | async-done | bytes 737296 | tf_op jit(solution)/shard_map/reduce_scatter | solution.py:99
  98.0 3.6 reshape.129
  101.5 5.6 scatter_custom_fusion
  107.1 73.7 %all_to_all.10 = bf16[8,64,2880]{2,1,0:T(8,128)(2,1)S(1)} all-to-all(bf16[8,64,2880]{2,1,0:T(8,128)(2,1)} %bitcast.63), channel_id=1, replica_groups=mesh['ctx'=4,'exp'=4,'head'=2] {'ctx','head'}, dimensions={0} | all-to-all | bytes 5898240 | tf_op jit(solution)/shard_map/all_to_all | solution.py:119
  183.9 66.3 %collective-permute-done.1 = bf16[8,64,2880]{2,1,0:T(8,128)(2,1)S(1)} collective-permute-done((bf16[8,64,2880]{2,1,0:T(8,128)(2,1)S(1)}, bf16[8,64,2880]{2,1,0:T(8,128)(2,1)S(1)}, u32[]{:S(2)}, u32[]{:S(2)}) %collective-permute-start.1) | collective-permute-done | bytes 2949152 | tf_op jit(solution)/shard_map/ppermute | solution.py:131
  252.3 66.4 %collective-permute-done.2 = bf16[8,64,2880]{2,1,0:T(8,128)(2,1)} collective-permute-done((bf16[8,64,2880]{2,1,0:T(8,128)(2,1)S(1)}, bf16[8,64,2880]{2,1,0:T(8,128)(2,1)}, u32[]{:S(2)}, u32[]{:S(2)}) %collective-permute-start.2) | collective-permute-done | bytes 2949152 | tf_op jit(solution)/shard_map/ppermute | solution.py:131
  318.7 6.1 broadcast_in_dim.40
  324.8 1.8 constant_dynamic-update-slice_fusion.5
  329.6 3.7 constant_dynamic-update-slice_fusion.3
  333.3 51.8 %collective-permute-done.3 = bf16[8,64,2880]{2,1,0:T(8,128)(2,1)} collective-permute-done((bf16[8,64,2880]{2,1,0:T(8,128)(2,1)}, bf16[8,64,2880]{2,1,0:T(8,128)(2,1)}, u32[]{:S(2)}, u32[]{:S(2)}) %collective-permute-start.3) | collective-permute-done | bytes 2949152 | tf_op jit(solution)/shard_map/ppermute | solution.py:131
  385.1 3.7 constant_dynamic-update-slice_fusion.2
  388.8 10.8 %fusion.7 = f32[2048,384]{1,0:T(8,128)S(1)} fusion(bf16[2048,2880]{1,0:T(8,128)(2,1)} %bitcast.61, bf16[1,2880,384]{2,1,0:T(8,128)(2,1)S(1)} %copy-done.11), kind=kOutput, calls=%fused_computation.9 | convolution fusion | flops 4529848320 | bytes 17154048 | tf_op jit(solution)/shard_map/dot_general | solution.py:61
  399.6 7.4 %multiply_convert_fusion = bf16[2048,384]{1,0:T(8,128)(2,1)S(1)} fusion(f32[2048,384]{1,0:T(8,128)S(1)} %fusion.7, bf16[2048,2880]{1,0:T(8,128)(2,1)S(1)} %bitcast.62, bf16[1,2880,384]{2,1,0:T(8,128)(2,1)S(1)} %copy-done.12), kind=kOutput, calls=%fused_computation.3 | convolution fusion | flops 4536139776 | bytes 18726912 | tf_op jit(solution)/shard_map/dot_general | solution.py:60
  407.1 11.4 %fusion.1 = f32[32,64,2880]{2,1,0:T(8,128)} fusion(bf16[32,64,384]{2,1,0:T(8,128)(2,1)S(1)} %bitcast.64, bf16[1,384,2880]{1,2,0:T(8,128)(2,1)S(1)} %copy-done), kind=kOutput, calls=%fused_computation.5 | convolution fusion | flops 4529848320 | bytes 27377664 | tf_op jit(solution)/shard_map/dot_general | solution.py:63
  418.5 212.6 %reduce-scatter.5.cloned.1.call-done = f32[8,64,2880]{2,1,0:T(8,128)} async-done(((f32[32,64,2880]{2,1,0:T(8,128)}), f32[8,64,2880]{2,1,0:T(8,128)}) %reduce-scatter.5.cloned.1.call-update) | async-done | bytes 5898256 | tf_op jit(solution)/shard_map/reduce_scatter | solution.py:135
  631.0 4.8 convert_element_type.48
  635.9 4.8 all-to-all-start.1
  640.8 68.6 %all-to-all-done.1 = bf16[8,64,2880]{2,1,0:T(8,128)(2,1)} async-done(((bf16[8,64,2880]{2,1,0:T(8,128)(2,1)}), bf16[8,64,2880]{2,1,0:T(8,128)(2,1)}, u32[]{:S(2)}, u32[]{:S(2)}) %all-to-all-start.1) | async-done | bytes 2949152 | tf_op jit(solution)/shard_map/all_to_all | solution.py:141
  709.4 6.4 gather_fusion
  715.8 3.9 reshape.116
  719.7 4.0 multiply_reduce_fusion
  (69 shorter events, 21.1 us)
Async XLA Ops:
  6.5 400.5 %copy-start = (bf16[1,384,2880]{1,2,0:T(8,128)(2,1)S(1)}, bf16[1,384,2880]{1,2,0:T(8,128)(2,1)}, u32[]{:S(2)}) copy-start(bf16[1,384,2880]{1,2,0:T(8,128)(2,1)} %param.21) | copy-start | bytes 6635524
  6.5 72.2 %all-gather.2.cloned.1.call-start = ((), (), s32[]{:S(2)}) async-start(), calls=%async_computation.4 | async-start | bytes 7372800 | tf_op jit(solution)/shard_map/all_gather | solution.py:96
  7.3 86.6 %reduce-scatter.3.cloned.1.call-start = ((), (), s32[]{:S(2)}) async-start(), calls=%async_computation.5 | async-start | bytes 2260992 | tf_op jit(solution)/shard_map/reduce_scatter | solution.py:99
  8.8 6.8 collective-permute-start
  78.7 6.1 copy-start.9
  78.7 15.1 %copy-start.5 = (bf16[64,2880]{1,0:T(8,128)(2,1)S(1)}, bf16[64,2880]{1,0:T(8,128)(2,1)}, u32[]{:S(2)}) copy-start(bf16[64,2880]{1,0:T(8,128)(2,1)} %param.14) | copy-start | bytes 1105924
  78.7 16.5 %copy-start.8 = (f32[2880]{0:T(1024)S(1)}, f32[2880]{0:T(1024)}, u32[]{:S(2)}) copy-start(f32[2880]{0:T(1024)} %param.16) | copy-start | bytes 34564
  84.7 546.3 %reduce-scatter.5.cloned.1.call-start = ((), (), s32[]{:S(2)}) async-start(), calls=%async_computation.6 | async-start | bytes 30146560 | tf_op jit(solution)/shard_map/reduce_scatter | solution.py:135
  180.8 1.6 copy-start.2
  182.4 67.7 %collective-permute-start.1 = (bf16[8,64,2880]{2,1,0:T(8,128)(2,1)S(1)}, bf16[8,64,2880]{2,1,0:T(8,128)(2,1)S(1)}, u32[]{:S(2)}, u32[]{:S(2)}) collective-permute-start(bf16[8,64,2880]{2,1,0:T(8,128)(2,1)S(1)} %all_to_all.10), channel_id=1, source_target_pairs={{0,2},{2,4},{4,6},{6,0},{1,3},{3,5},{5,7},{7,1},{8,10},{10,12},{12... | collective-permute-start | bytes 8847368 | tf_op jit(solution)/shard_map/ppermute | solution.py:131
  250.2 1.6 copy-start.6
  251.7 67.0 %collective-permute-start.2 = (bf16[8,64,2880]{2,1,0:T(8,128)(2,1)S(1)}, bf16[8,64,2880]{2,1,0:T(8,128)(2,1)}, u32[]{:S(2)}, u32[]{:S(2)}) collective-permute-start(bf16[8,64,2880]{2,1,0:T(8,128)(2,1)S(1)} %collective-permute-done.1), channel_id=1, source_target_pairs={{0,2},{2,4},{4,6},{6,0},{1,3},{3,5},{5,7},{7,1},{8,10},{10,12},{12... | collective-permute-start | bytes 8847368 | tf_op jit(solution)/shard_map/ppermute | solution.py:131
  318.7 66.3 %collective-permute-start.3 = (bf16[8,64,2880]{2,1,0:T(8,128)(2,1)}, bf16[8,64,2880]{2,1,0:T(8,128)(2,1)}, u32[]{:S(2)}, u32[]{:S(2)}) collective-permute-start(bf16[8,64,2880]{2,1,0:T(8,128)(2,1)} %collective-permute-done.2), channel_id=1, source_target_pairs={{0,2},{2,4},{4,6},{6,0},{1,3},{3,5},{5,7},{7,1},{8,10},{10,12},{12... | collective-permute-start | bytes 8847368 | tf_op jit(solution)/shard_map/ppermute | solution.py:131
  318.7 6.1 copy-start.3
  324.8 2.9 copy-start.7
  333.3 55.5 %copy-start.11 = (bf16[1,2880,384]{2,1,0:T(8,128)(2,1)S(1)}, bf16[1,2880,384]{2,1,0:T(8,128)(2,1)}, u32[]{:S(2)}) copy-start(bf16[1,2880,384]{2,1,0:T(8,128)(2,1)} %param.20) | copy-start | bytes 6635524
  388.8 10.8 %copy-start.1 = (bf16[32,64,2880]{2,1,0:T(8,128)(2,1)S(1)}, bf16[32,64,2880]{2,1,0:T(8,128)(2,1)}, u32[]{:S(2)}) copy-start(bf16[32,64,2880]{2,1,0:T(8,128)(2,1)} %constant_dynamic-update-slice_fusion.2) | copy-start | bytes 35389444
  388.8 10.8 %copy-start.12 = (bf16[1,2880,384]{2,1,0:T(8,128)(2,1)S(1)}, bf16[1,2880,384]{2,1,0:T(8,128)(2,1)}, u32[]{:S(2)}) copy-start(bf16[1,2880,384]{2,1,0:T(8,128)(2,1)} %param.19) | copy-start | bytes 6635524
  635.9 4.8 copy-start.10
  635.9 73.5 %all-to-all-start.1 = ((bf16[8,64,2880]{2,1,0:T(8,128)(2,1)}), bf16[8,64,2880]{2,1,0:T(8,128)(2,1)}, u32[]{:S(2)}, u32[]{:S(2)}) async-start(bf16[8,64,2880]{2,1,0:T(8,128)(2,1)} %convert_element_type.48), calls=%async_computation.3 | async-start | bytes 6029312 | tf_op jit(solution)/shard_map/all_to_all | solution.py:141
  719.7 4.0 copy-start.4
Sparse Core Ops, SparseCore 0:
  9.2 69.4 all-gather.1
  84.8 8.9 reduce-scatter.2
  418.6 212.3 reduce-scatter.4
